TPU v7x, 32 devices: a whole 2x2x4 slice. The times are simulated.
32 devices in a mesh: comp: 2 (over core), tile: 16 (over z, y, x).
Axes of the slice: x: 2, y: 2, z: 4, core: 2. Of those that a mesh axis runs over, the one named last changes fastest.
Arguments:
- tracer: float32 [2, 16, 4, 64, 1024], P('comp', None, None, 'tile'), may hold values from -6 to 6
- velocity: float32 [2, 2, 4, 64, 1024], P('comp', None, None, 'tile'), may hold values from -0.3 to 0.3
- coupling: float32 [2, 16, 64, 1024], P('comp', None, 'tile'), may hold values from 0.05 to 0.5
- sea_mask: int32 [2, 64, 1024], P('comp', 'tile'), may hold values 0 or 1
- send_rows: int32 [2, 16, 4, 2048], P('comp', 'tile'), may hold values from 0 to 3
- send_cols: int32 [2, 16, 4, 2048], P('comp', 'tile'), may hold values from 0 to 1023
- intersection_near: int32 [2, 8, 64, 1024], P('comp', None, 'tile'), may hold values from 0 to 3
- intersection_slot: int32 [2, 8, 64, 1024], P('comp', None, 'tile'), may hold values from 0 to 2047
- intersection_weight: float32 [2, 8, 64, 1024], P('comp', None, 'tile'), as said below
Outputs:
- tracer_out: float32 [2, 16, 4, 64, 1024], P('comp', None, None, 'tile')
Inputs may be any that keep to these rules, and one draw needn't show every extreme that they name: `intersection_weight`: positive, summing to one over the 8 intersections of a cell.
All inputs are finite; a program needn't handle non-finite values. No bound on the sum of `sea_mask` on one device may be relied on, other than what follows from the above.
Results may differ from a plain program's by a relative error of at most 0.000088.
Values sent between devices are 32-bit elements; how exact they have to be, the bound alone decides.
A program may use at most 64 MiB of HBM per device.

v0:
```python
import math

import jax
import jax.numpy as jnp
from jax import lax
from jax.sharding import PartitionSpec as P

diffusion = 0.12


def swapped(value, axis, bit):
    mask = 2**bit
    pairs = [(source, source ^ mask) for source in range(lax.axis_size(axis))]
    return lax.ppermute(value, axis, pairs)


def passed_along(value, axis, steps):
    count = lax.axis_size(axis)
    pairs = [(source, (source + steps) % count) for source in range(count)]
    return lax.ppermute(value, axis, pairs)


def with_halo(x, sides, width):
    for axis, dim in sides:
        devices, length = (lax.axis_size(axis), x.shape[dim])
        up = [(i, (i + 1) % devices) for i in range(devices)]
        down = [(j, i) for i, j in up]
        last = lax.slice_in_dim(x, length - width, length, axis=dim)
        first = lax.slice_in_dim(x, 0, width, axis=dim)
        before = lax.ppermute(last, axis, up)
        after = lax.ppermute(first, axis, down)
        x = jnp.concatenate([before, x, after], axis=dim)
    return x


def substep(padded, speed):
    field = padded[:, :, 1:-1]
    east = padded[:, :, 2:]
    west = padded[:, :, :-2]
    north = jnp.roll(field, -1, axis=3)
    south = jnp.roll(field, 1, axis=3)
    return (
        field
        - 0.5 * speed[0] * (east - west)
        - 0.5 * speed[1] * (north - south)
        + diffusion * (east + west + north + south - 4.0 * field)
    )


def pack_rows(surface, rows, cols):
    tracers, rows_x, width = surface.shape
    neighbours, capacity = rows.shape
    total_slots = neighbours * capacity
    block = math.gcd(total_slots, 1024)
    count = total_slots // block
    row_blocks = rows.reshape(count, block)
    col_blocks = cols.reshape(count, block)

    def pack_one_block(pair):
        row_ids, col_ids = pair
        col_hot = (lax.broadcasted_iota(jnp.int32, (width, block), 0) == col_ids[None, :]).astype(
            jnp.float32
        )
        partial_rows = jnp.einsum(
            "qry,ys->qrs",
            surface,
            col_hot,
            precision=lax.Precision.HIGHEST,
            preferred_element_type=jnp.float32,
        )
        row_hot = (lax.broadcasted_iota(jnp.int32, (rows_x, block), 0) == row_ids[None, :]).astype(
            jnp.float32
        )
        return jnp.sum(partial_rows * row_hot[None], axis=1)

    packed = lax.map(pack_one_block, (row_blocks, col_blocks))
    return jnp.transpose(packed, (1, 0, 2)).reshape(tracers, neighbours, capacity)


def per_device(
    tracer,
    velocity,
    coupling,
    sea_mask,
    send_rows,
    send_cols,
    intersection_near,
    intersection_slot,
    intersection_weight,
):
    field = tracer[0]
    speed = velocity[0]
    tracers, levels, rows_x, width = field.shape
    neighbours = send_rows.shape[2]
    capacity = send_rows.shape[3]
    intersections = intersection_slot.shape[1]
    cells = rows_x * width
    surface = field[:, 0]
    cell_block = math.gcd(cells, 512)
    cell_count = cells // cell_block
    near_blocks = jnp.transpose(
        intersection_near[0].reshape(intersections, cell_count, cell_block), (1, 0, 2)
    )
    slot_blocks = jnp.transpose(
        intersection_slot[0].reshape(intersections, cell_count, cell_block), (1, 0, 2)
    )
    weight_blocks = jnp.transpose(
        intersection_weight[0].reshape(intersections, cell_count, cell_block), (1, 0, 2)
    )
    other_surface = swapped(surface, "comp", 0)
    other_rows, other_cols = swapped((send_rows[0, 0], send_cols[0, 0]), "comp", 0)
    packed = pack_rows(other_surface, other_rows, other_cols)
    pieces = []
    for near in range(neighbours):
        pieces.append(passed_along(packed[:, near], "tile", 1 - near))
    received = jnp.stack(pieces, axis=1)

    def remap_one_block(triple):
        near_ids, slot_ids, weight_vals = triple
        positions = lax.broadcasted_iota(jnp.int32, (capacity, cell_block), 0)
        total = jnp.zeros((tracers, cell_block), jnp.float32)
        for near in range(neighbours):
            table = jnp.zeros((capacity, cell_block), jnp.float32)
            for k in range(intersections):
                hit = (positions == slot_ids[k][None, :]) & (near_ids[k][None, :] == near)
                table = table + jnp.where(hit, weight_vals[k][None, :], 0.0)
            total = total + jnp.dot(
                received[:, near],
                table,
                precision=lax.Precision.HIGHEST,
                preferred_element_type=jnp.float32,
            )
        return total

    blocks = lax.map(remap_one_block, (near_blocks, slot_blocks, weight_blocks))
    remapped = jnp.transpose(blocks, (1, 0, 2)).reshape(tracers, rows_x, width)
    level0 = field[:, 0]
    masked = sea_mask[0].astype(jnp.float32)
    new0 = level0 + coupling[0] * masked * (remapped - level0)
    field = field.at[:, 0].set(new0)
    for step in range(2):
        padded = with_halo(field, (("tile", 2),), 1)
        field = substep(padded, speed)
    return field[None]


def solution(mesh):
    in_specs = (
        P("comp", None, None, "tile", None),
        P("comp", None, None, "tile", None),
        P("comp", None, "tile", None),
        P("comp", "tile", None),
        P("comp", "tile", None, None),
        P("comp", "tile", None, None),
        P("comp", None, "tile", None),
        P("comp", None, "tile", None),
        P("comp", None, "tile", None),
    )
    out_specs = P("comp", None, None, "tile", None)
    return jax.shard_map(
        per_device, mesh=mesh, in_specs=in_specs, out_specs=out_specs, check_vma=False
    )
```

profile of v0, /device:TPU:0, one launch (start us, length us, event | category | flops | bytes accessed | tf_op | source)
XLA Modules:
  0.0 373.4 jit_solution(7739083732666481892)
XLA Ops:
  4.5 13.5 %while.21 = (s32[]{:T(128)}, f32[8,16,1024]{2,1,0:T(8,128)S(1)}, s32[8,1024]{1,0:T(8,128)S(1)}, f32[16,4,1024]{2,0,1:T(8,128)S(1)}, s32[8,1024]{1,0:T(8,128)S(1)}, /*index=5*/s32[]{:T(128)}) while((s32[]{:T(128)}, f32[8,16,1024]{2,1,0:T(8,128)S(1)}, s32[8,1024]{1,0:T(8,128)S(1)}, f32[16,4,1024]{2,0,1:T(8,128)S(1)}, s32[8,1024]{1,0:T(8,128)S(1)}, ...), condition=%wide.region_2.3_spmd, body=%wide.region_0.2_spmd.sunk | while | flops 806477824 | bytes 516181 | solution.py:76
  4.5 1.6 fusion.303
  6.2 1.6 fusion.303
  7.9 1.6 fusion.303
  11.3 1.6 fusion.303
  19.2 2.8 collective-permute-start.3
  22.0 4.1 %collective-permute-start.5 = (f32[16,2048]{1,0:T(8,128)S(1)}, f32[16,2048]{1,0:T(8,128)S(1)}, u32[]{:S(2)}, u32[]{:S(2)}) collective-permute-start(f32[16,2048]{1,0:T(8,128)S(1)} %bitcast.261), channel_id=1, source_target_pairs={{0,15},{1,0},{2,1},{3,2},{4,3},{5,4},{6,5},{7,6},{8,7},{9,8},{10,9... | collective-permute-start | bytes 393224 | tf_op jit(solution)/shard_map/ppermute | solution.py:20
  26.1 2.0 collective-permute-start.6
  30.2 2.7 collective-permute-done.6
  32.9 306.0 %while.22 = (s32[]{:T(128)}, f32[8,16,512]{2,1,0:T(8,128)S(1)}, s32[8,8,512]{2,0,1:T(8,128)S(1)}, s32[8,8,512]{2,0,1:T(8,128)S(1)}, f32[8,8,512]{2,0,1:T(8,128)S...) while((s32[]{:T(128)}, f32[8,16,512]{2,1,0:T(8,128)S(1)}, ...), condition=%wide.region_4.5_spmd, body=%wide.region_3.4_spmd.sunk | while | flops 935370752 | bytes 999781 | solution.py:135
  33.2 9.5 %fusion.312 = f32[512,16]{0,1:T(8,128)S(1)} fusion(f32[16,2048]{1,0:T(8,128)S(1)} %get-tuple-element.456, f32[512]{0:T(512)S(1)} %bitcast.293, s32[512]{0:T(512)S(1)} %bitcast.325, f32[512]{0:T(512)S(1)} %bitcast.269, s32[512]{0:T(512)S(1)} %bitcast.301, f32[512]{0:T(512)S(1)} %bitcast.273, s32[512]{0:T(512)S(1)} %bitcast.305, ...), kind=kOutput, calls=%fused_computation.12.clone.1 | convolution fusion | flops 233832448 | bytes 200704 | tf_op jit(solution)/shard_map/while/body/eval_jaxpr/dot_general | solution.py:127
  42.6 9.5 %fusion.313 = f32[512,16]{0,1:T(8,128)S(1)} fusion(f32[16,2048]{1,0:T(8,128)S(1)} %get-tuple-element.455, f32[512]{0:T(512)S(1)} %bitcast.294, s32[512]{0:T(512)S(1)} %bitcast.326, f32[512]{0:T(512)S(1)} %bitcast.270, s32[512]{0:T(512)S(1)} %bitcast.302, f32[512]{0:T(512)S(1)} %bitcast.274, s32[512]{0:T(512)S(1)} %bitcast.306, ...), kind=kOutput, calls=%fused_computation.28.clone.1 | convolution fusion | flops 233832448 | bytes 200704 | tf_op jit(solution)/shard_map/while/body/eval_jaxpr/dot_general | solution.py:127
  52.1 9.5 %fusion.314 = f32[512,16]{0,1:T(8,128)S(1)} fusion(f32[16,2048]{1,0:T(8,128)S(1)} %get-tuple-element.454, f32[512]{0:T(512)S(1)} %bitcast.295, s32[512]{0:T(512)S(1)} %bitcast.327, f32[512]{0:T(512)S(1)} %bitcast.271, s32[512]{0:T(512)S(1)} %bitcast.303, f32[512]{0:T(512)S(1)} %bitcast.275, s32[512]{0:T(512)S(1)} %bitcast.307, ...), kind=kOutput, calls=%fused_computation.44.clone.1 | convolution fusion | flops 233832448 | bytes 200704 | tf_op jit(solution)/shard_map/while/body/eval_jaxpr/dot_general | solution.py:127
  61.6 9.5 %fusion.315 = f32[8,16,512]{2,1,0:T(8,128)S(1)} fusion(f32[8,16,512]{2,1,0:T(8,128)S(1)} %get-tuple-element.431, s32[]{:T(128)S(6)} %copy.67, f32[512,16]{0,1:T(8,128)S(1)} %fusion.312, f32[512,16]{0,1:T(8,128)S(1)} %fusion.313, f32[512,16]{0,1:T(8,128)S(1)} %fusion.314, f32[16,2048]{1,0:T(8,128)S(1)} %get-tuple-element.453, f32[512]{0:T(512)S(1)} %bitcast.296, ...), kind=kOutput, calls=%fused_computation.220.clone.1 | convolution fusion | flops 233857024 | bytes 299012 | tf_op jit(solution)/shard_map/while/body/eval_jaxpr/dot_general | solution.py:127
  71.4 9.5 %fusion.312 = f32[512,16]{0,1:T(8,128)S(1)} fusion(f32[16,2048]{1,0:T(8,128)S(1)} %get-tuple-element.456, f32[512]{0:T(512)S(1)} %bitcast.293, s32[512]{0:T(512)S(1)} %bitcast.325, f32[512]{0:T(512)S(1)} %bitcast.269, s32[512]{0:T(512)S(1)} %bitcast.301, f32[512]{0:T(512)S(1)} %bitcast.273, s32[512]{0:T(512)S(1)} %bitcast.305, ...), kind=kOutput, calls=%fused_computation.12.clone.1 | convolution fusion | flops 233832448 | bytes 200704 | tf_op jit(solution)/shard_map/while/body/eval_jaxpr/dot_general | solution.py:127
  80.9 9.5 %fusion.313 = f32[512,16]{0,1:T(8,128)S(1)} fusion(f32[16,2048]{1,0:T(8,128)S(1)} %get-tuple-element.455, f32[512]{0:T(512)S(1)} %bitcast.294, s32[512]{0:T(512)S(1)} %bitcast.326, f32[512]{0:T(512)S(1)} %bitcast.270, s32[512]{0:T(512)S(1)} %bitcast.302, f32[512]{0:T(512)S(1)} %bitcast.274, s32[512]{0:T(512)S(1)} %bitcast.306, ...), kind=kOutput, calls=%fused_computation.28.clone.1 | convolution fusion | flops 233832448 | bytes 200704 | tf_op jit(solution)/shard_map/while/body/eval_jaxpr/dot_general | solution.py:127
  90.3 9.5 %fusion.314 = f32[512,16]{0,1:T(8,128)S(1)} fusion(f32[16,2048]{1,0:T(8,128)S(1)} %get-tuple-element.454, f32[512]{0:T(512)S(1)} %bitcast.295, s32[512]{0:T(512)S(1)} %bitcast.327, f32[512]{0:T(512)S(1)} %bitcast.271, s32[512]{0:T(512)S(1)} %bitcast.303, f32[512]{0:T(512)S(1)} %bitcast.275, s32[512]{0:T(512)S(1)} %bitcast.307, ...), kind=kOutput, calls=%fused_computation.44.clone.1 | convolution fusion | flops 233832448 | bytes 200704 | tf_op jit(solution)/shard_map/while/body/eval_jaxpr/dot_general | solution.py:127
  99.8 9.5 %fusion.315 = f32[8,16,512]{2,1,0:T(8,128)S(1)} fusion(f32[8,16,512]{2,1,0:T(8,128)S(1)} %get-tuple-element.431, s32[]{:T(128)S(6)} %copy.67, f32[512,16]{0,1:T(8,128)S(1)} %fusion.312, f32[512,16]{0,1:T(8,128)S(1)} %fusion.313, f32[512,16]{0,1:T(8,128)S(1)} %fusion.314, f32[16,2048]{1,0:T(8,128)S(1)} %get-tuple-element.453, f32[512]{0:T(512)S(1)} %bitcast.296, ...), kind=kOutput, calls=%fused_computation.220.clone.1 | convolution fusion | flops 233857024 | bytes 299012 | tf_op jit(solution)/shard_map/while/body/eval_jaxpr/dot_general | solution.py:127
  109.6 9.5 %fusion.312 = f32[512,16]{0,1:T(8,128)S(1)} fusion(f32[16,2048]{1,0:T(8,128)S(1)} %get-tuple-element.456, f32[512]{0:T(512)S(1)} %bitcast.293, s32[512]{0:T(512)S(1)} %bitcast.325, f32[512]{0:T(512)S(1)} %bitcast.269, s32[512]{0:T(512)S(1)} %bitcast.301, f32[512]{0:T(512)S(1)} %bitcast.273, s32[512]{0:T(512)S(1)} %bitcast.305, ...), kind=kOutput, calls=%fused_computation.12.clone.1 | convolution fusion | flops 233832448 | bytes 200704 | tf_op jit(solution)/shard_map/while/body/eval_jaxpr/dot_general | solution.py:127
  119.1 9.5 %fusion.313 = f32[512,16]{0,1:T(8,128)S(1)} fusion(f32[16,2048]{1,0:T(8,128)S(1)} %get-tuple-element.455, f32[512]{0:T(512)S(1)} %bitcast.294, s32[512]{0:T(512)S(1)} %bitcast.326, f32[512]{0:T(512)S(1)} %bitcast.270, s32[512]{0:T(512)S(1)} %bitcast.302, f32[512]{0:T(512)S(1)} %bitcast.274, s32[512]{0:T(512)S(1)} %bitcast.306, ...), kind=kOutput, calls=%fused_computation.28.clone.1 | convolution fusion | flops 233832448 | bytes 200704 | tf_op jit(solution)/shard_map/while/body/eval_jaxpr/dot_general | solution.py:127
  128.6 9.5 %fusion.314 = f32[512,16]{0,1:T(8,128)S(1)} fusion(f32[16,2048]{1,0:T(8,128)S(1)} %get-tuple-element.454, f32[512]{0:T(512)S(1)} %bitcast.295, s32[512]{0:T(512)S(1)} %bitcast.327, f32[512]{0:T(512)S(1)} %bitcast.271, s32[512]{0:T(512)S(1)} %bitcast.303, f32[512]{0:T(512)S(1)} %bitcast.275, s32[512]{0:T(512)S(1)} %bitcast.307, ...), kind=kOutput, calls=%fused_computation.44.clone.1 | convolution fusion | flops 233832448 | bytes 200704 | tf_op jit(solution)/shard_map/while/body/eval_jaxpr/dot_general | solution.py:127
  138.0 9.5 %fusion.315 = f32[8,16,512]{2,1,0:T(8,128)S(1)} fusion(f32[8,16,512]{2,1,0:T(8,128)S(1)} %get-tuple-element.431, s32[]{:T(128)S(6)} %copy.67, f32[512,16]{0,1:T(8,128)S(1)} %fusion.312, f32[512,16]{0,1:T(8,128)S(1)} %fusion.313, f32[512,16]{0,1:T(8,128)S(1)} %fusion.314, f32[16,2048]{1,0:T(8,128)S(1)} %get-tuple-element.453, f32[512]{0:T(512)S(1)} %bitcast.296, ...), kind=kOutput, calls=%fused_computation.220.clone.1 | convolution fusion | flops 233857024 | bytes 299012 | tf_op jit(solution)/shard_map/while/body/eval_jaxpr/dot_general | solution.py:127
  147.8 9.5 %fusion.312 = f32[512,16]{0,1:T(8,128)S(1)} fusion(f32[16,2048]{1,0:T(8,128)S(1)} %get-tuple-element.456, f32[512]{0:T(512)S(1)} %bitcast.293, s32[512]{0:T(512)S(1)} %bitcast.325, f32[512]{0:T(512)S(1)} %bitcast.269, s32[512]{0:T(512)S(1)} %bitcast.301, f32[512]{0:T(512)S(1)} %bitcast.273, s32[512]{0:T(512)S(1)} %bitcast.305, ...), kind=kOutput, calls=%fused_computation.12.clone.1 | convolution fusion | flops 233832448 | bytes 200704 | tf_op jit(solution)/shard_map/while/body/eval_jaxpr/dot_general | solution.py:127
  157.3 9.5 %fusion.313 = f32[512,16]{0,1:T(8,128)S(1)} fusion(f32[16,2048]{1,0:T(8,128)S(1)} %get-tuple-element.455, f32[512]{0:T(512)S(1)} %bitcast.294, s32[512]{0:T(512)S(1)} %bitcast.326, f32[512]{0:T(512)S(1)} %bitcast.270, s32[512]{0:T(512)S(1)} %bitcast.302, f32[512]{0:T(512)S(1)} %bitcast.274, s32[512]{0:T(512)S(1)} %bitcast.306, ...), kind=kOutput, calls=%fused_computation.28.clone.1 | convolution fusion | flops 233832448 | bytes 200704 | tf_op jit(solution)/shard_map/while/body/eval_jaxpr/dot_general | solution.py:127
  166.8 9.5 %fusion.314 = f32[512,16]{0,1:T(8,128)S(1)} fusion(f32[16,2048]{1,0:T(8,128)S(1)} %get-tuple-element.454, f32[512]{0:T(512)S(1)} %bitcast.295, s32[512]{0:T(512)S(1)} %bitcast.327, f32[512]{0:T(512)S(1)} %bitcast.271, s32[512]{0:T(512)S(1)} %bitcast.303, f32[512]{0:T(512)S(1)} %bitcast.275, s32[512]{0:T(512)S(1)} %bitcast.307, ...), kind=kOutput, calls=%fused_computation.44.clone.1 | convolution fusion | flops 233832448 | bytes 200704 | tf_op jit(solution)/shard_map/while/body/eval_jaxpr/dot_general | solution.py:127
  176.3 9.5 %fusion.315 = f32[8,16,512]{2,1,0:T(8,128)S(1)} fusion(f32[8,16,512]{2,1,0:T(8,128)S(1)} %get-tuple-element.431, s32[]{:T(128)S(6)} %copy.67, f32[512,16]{0,1:T(8,128)S(1)} %fusion.312, f32[512,16]{0,1:T(8,128)S(1)} %fusion.313, f32[512,16]{0,1:T(8,128)S(1)} %fusion.314, f32[16,2048]{1,0:T(8,128)S(1)} %get-tuple-element.453, f32[512]{0:T(512)S(1)} %bitcast.296, ...), kind=kOutput, calls=%fused_computation.220.clone.1 | convolution fusion | flops 233857024 | bytes 299012 | tf_op jit(solution)/shard_map/while/body/eval_jaxpr/dot_general | solution.py:127
  186.1 9.5 %fusion.312 = f32[512,16]{0,1:T(8,128)S(1)} fusion(f32[16,2048]{1,0:T(8,128)S(1)} %get-tuple-element.456, f32[512]{0:T(512)S(1)} %bitcast.293, s32[512]{0:T(512)S(1)} %bitcast.325, f32[512]{0:T(512)S(1)} %bitcast.269, s32[512]{0:T(512)S(1)} %bitcast.301, f32[512]{0:T(512)S(1)} %bitcast.273, s32[512]{0:T(512)S(1)} %bitcast.305, ...), kind=kOutput, calls=%fused_computation.12.clone.1 | convolution fusion | flops 233832448 | bytes 200704 | tf_op jit(solution)/shard_map/while/body/eval_jaxpr/dot_general | solution.py:127
  195.5 9.5 %fusion.313 = f32[512,16]{0,1:T(8,128)S(1)} fusion(f32[16,2048]{1,0:T(8,128)S(1)} %get-tuple-element.455, f32[512]{0:T(512)S(1)} %bitcast.294, s32[512]{0:T(512)S(1)} %bitcast.326, f32[512]{0:T(512)S(1)} %bitcast.270, s32[512]{0:T(512)S(1)} %bitcast.302, f32[512]{0:T(512)S(1)} %bitcast.274, s32[512]{0:T(512)S(1)} %bitcast.306, ...), kind=kOutput, calls=%fused_computation.28.clone.1 | convolution fusion | flops 233832448 | bytes 200704 | tf_op jit(solution)/shard_map/while/body/eval_jaxpr/dot_general | solution.py:127
  205.0 9.5 %fusion.314 = f32[512,16]{0,1:T(8,128)S(1)} fusion(f32[16,2048]{1,0:T(8,128)S(1)} %get-tuple-element.454, f32[512]{0:T(512)S(1)} %bitcast.295, s32[512]{0:T(512)S(1)} %bitcast.327, f32[512]{0:T(512)S(1)} %bitcast.271, s32[512]{0:T(512)S(1)} %bitcast.303, f32[512]{0:T(512)S(1)} %bitcast.275, s32[512]{0:T(512)S(1)} %bitcast.307, ...), kind=kOutput, calls=%fused_computation.44.clone.1 | convolution fusion | flops 233832448 | bytes 200704 | tf_op jit(solution)/shard_map/while/body/eval_jaxpr/dot_general | solution.py:127
  214.5 9.5 %fusion.315 = f32[8,16,512]{2,1,0:T(8,128)S(1)} fusion(f32[8,16,512]{2,1,0:T(8,128)S(1)} %get-tuple-element.431, s32[]{:T(128)S(6)} %copy.67, f32[512,16]{0,1:T(8,128)S(1)} %fusion.312, f32[512,16]{0,1:T(8,128)S(1)} %fusion.313, f32[512,16]{0,1:T(8,128)S(1)} %fusion.314, f32[16,2048]{1,0:T(8,128)S(1)} %get-tuple-element.453, f32[512]{0:T(512)S(1)} %bitcast.296, ...), kind=kOutput, calls=%fused_computation.220.clone.1 | convolution fusion | flops 233857024 | bytes 299012 | tf_op jit(solution)/shard_map/while/body/eval_jaxpr/dot_general | solution.py:127
  224.3 9.5 %fusion.312 = f32[512,16]{0,1:T(8,128)S(1)} fusion(f32[16,2048]{1,0:T(8,128)S(1)} %get-tuple-element.456, f32[512]{0:T(512)S(1)} %bitcast.293, s32[512]{0:T(512)S(1)} %bitcast.325, f32[512]{0:T(512)S(1)} %bitcast.269, s32[512]{0:T(512)S(1)} %bitcast.301, f32[512]{0:T(512)S(1)} %bitcast.273, s32[512]{0:T(512)S(1)} %bitcast.305, ...), kind=kOutput, calls=%fused_computation.12.clone.1 | convolution fusion | flops 233832448 | bytes 200704 | tf_op jit(solution)/shard_map/while/body/eval_jaxpr/dot_general | solution.py:127
  233.8 9.5 %fusion.313 = f32[512,16]{0,1:T(8,128)S(1)} fusion(f32[16,2048]{1,0:T(8,128)S(1)} %get-tuple-element.455, f32[512]{0:T(512)S(1)} %bitcast.294, s32[512]{0:T(512)S(1)} %bitcast.326, f32[512]{0:T(512)S(1)} %bitcast.270, s32[512]{0:T(512)S(1)} %bitcast.302, f32[512]{0:T(512)S(1)} %bitcast.274, s32[512]{0:T(512)S(1)} %bitcast.306, ...), kind=kOutput, calls=%fused_computation.28.clone.1 | convolution fusion | flops 233832448 | bytes 200704 | tf_op jit(solution)/shard_map/while/body/eval_jaxpr/dot_general | solution.py:127
  243.2 9.5 %fusion.314 = f32[512,16]{0,1:T(8,128)S(1)} fusion(f32[16,2048]{1,0:T(8,128)S(1)} %get-tuple-element.454, f32[512]{0:T(512)S(1)} %bitcast.295, s32[512]{0:T(512)S(1)} %bitcast.327, f32[512]{0:T(512)S(1)} %bitcast.271, s32[512]{0:T(512)S(1)} %bitcast.303, f32[512]{0:T(512)S(1)} %bitcast.275, s32[512]{0:T(512)S(1)} %bitcast.307, ...), kind=kOutput, calls=%fused_computation.44.clone.1 | convolution fusion | flops 233832448 | bytes 200704 | tf_op jit(solution)/shard_map/while/body/eval_jaxpr/dot_general | solution.py:127
  252.7 9.5 %fusion.315 = f32[8,16,512]{2,1,0:T(8,128)S(1)} fusion(f32[8,16,512]{2,1,0:T(8,128)S(1)} %get-tuple-element.431, s32[]{:T(128)S(6)} %copy.67, f32[512,16]{0,1:T(8,128)S(1)} %fusion.312, f32[512,16]{0,1:T(8,128)S(1)} %fusion.313, f32[512,16]{0,1:T(8,128)S(1)} %fusion.314, f32[16,2048]{1,0:T(8,128)S(1)} %get-tuple-element.453, f32[512]{0:T(512)S(1)} %bitcast.296, ...), kind=kOutput, calls=%fused_computation.220.clone.1 | convolution fusion | flops 233857024 | bytes 299012 | tf_op jit(solution)/shard_map/while/body/eval_jaxpr/dot_general | solution.py:127
  262.5 9.5 %fusion.312 = f32[512,16]{0,1:T(8,128)S(1)} fusion(f32[16,2048]{1,0:T(8,128)S(1)} %get-tuple-element.456, f32[512]{0:T(512)S(1)} %bitcast.293, s32[512]{0:T(512)S(1)} %bitcast.325, f32[512]{0:T(512)S(1)} %bitcast.269, s32[512]{0:T(512)S(1)} %bitcast.301, f32[512]{0:T(512)S(1)} %bitcast.273, s32[512]{0:T(512)S(1)} %bitcast.305, ...), kind=kOutput, calls=%fused_computation.12.clone.1 | convolution fusion | flops 233832448 | bytes 200704 | tf_op jit(solution)/shard_map/while/body/eval_jaxpr/dot_general | solution.py:127
  272.0 9.5 %fusion.313 = f32[512,16]{0,1:T(8,128)S(1)} fusion(f32[16,2048]{1,0:T(8,128)S(1)} %get-tuple-element.455, f32[512]{0:T(512)S(1)} %bitcast.294, s32[512]{0:T(512)S(1)} %bitcast.326, f32[512]{0:T(512)S(1)} %bitcast.270, s32[512]{0:T(512)S(1)} %bitcast.302, f32[512]{0:T(512)S(1)} %bitcast.274, s32[512]{0:T(512)S(1)} %bitcast.306, ...), kind=kOutput, calls=%fused_computation.28.clone.1 | convolution fusion | flops 233832448 | bytes 200704 | tf_op jit(solution)/shard_map/while/body/eval_jaxpr/dot_general | solution.py:127
  281.5 9.5 %fusion.314 = f32[512,16]{0,1:T(8,128)S(1)} fusion(f32[16,2048]{1,0:T(8,128)S(1)} %get-tuple-element.454, f32[512]{0:T(512)S(1)} %bitcast.295, s32[512]{0:T(512)S(1)} %bitcast.327, f32[512]{0:T(512)S(1)} %bitcast.271, s32[512]{0:T(512)S(1)} %bitcast.303, f32[512]{0:T(512)S(1)} %bitcast.275, s32[512]{0:T(512)S(1)} %bitcast.307, ...), kind=kOutput, calls=%fused_computation.44.clone.1 | convolution fusion | flops 233832448 | bytes 200704 | tf_op jit(solution)/shard_map/while/body/eval_jaxpr/dot_general | solution.py:127
  290.9 9.5 %fusion.315 = f32[8,16,512]{2,1,0:T(8,128)S(1)} fusion(f32[8,16,512]{2,1,0:T(8,128)S(1)} %get-tuple-element.431, s32[]{:T(128)S(6)} %copy.67, f32[512,16]{0,1:T(8,128)S(1)} %fusion.312, f32[512,16]{0,1:T(8,128)S(1)} %fusion.313, f32[512,16]{0,1:T(8,128)S(1)} %fusion.314, f32[16,2048]{1,0:T(8,128)S(1)} %get-tuple-element.453, f32[512]{0:T(512)S(1)} %bitcast.296, ...), kind=kOutput, calls=%fused_computation.220.clone.1 | convolution fusion | flops 233857024 | bytes 299012 | tf_op jit(solution)/shard_map/while/body/eval_jaxpr/dot_general | solution.py:127
  300.7 9.5 %fusion.312 = f32[512,16]{0,1:T(8,128)S(1)} fusion(f32[16,2048]{1,0:T(8,128)S(1)} %get-tuple-element.456, f32[512]{0:T(512)S(1)} %bitcast.293, s32[512]{0:T(512)S(1)} %bitcast.325, f32[512]{0:T(512)S(1)} %bitcast.269, s32[512]{0:T(512)S(1)} %bitcast.301, f32[512]{0:T(512)S(1)} %bitcast.273, s32[512]{0:T(512)S(1)} %bitcast.305, ...), kind=kOutput, calls=%fused_computation.12.clone.1 | convolution fusion | flops 233832448 | bytes 200704 | tf_op jit(solution)/shard_map/while/body/eval_jaxpr/dot_general | solution.py:127
  310.2 9.5 %fusion.313 = f32[512,16]{0,1:T(8,128)S(1)} fusion(f32[16,2048]{1,0:T(8,128)S(1)} %get-tuple-element.455, f32[512]{0:T(512)S(1)} %bitcast.294, s32[512]{0:T(512)S(1)} %bitcast.326, f32[512]{0:T(512)S(1)} %bitcast.270, s32[512]{0:T(512)S(1)} %bitcast.302, f32[512]{0:T(512)S(1)} %bitcast.274, s32[512]{0:T(512)S(1)} %bitcast.306, ...), kind=kOutput, calls=%fused_computation.28.clone.1 | convolution fusion | flops 233832448 | bytes 200704 | tf_op jit(solution)/shard_map/while/body/eval_jaxpr/dot_general | solution.py:127
  319.7 9.5 %fusion.314 = f32[512,16]{0,1:T(8,128)S(1)} fusion(f32[16,2048]{1,0:T(8,128)S(1)} %get-tuple-element.454, f32[512]{0:T(512)S(1)} %bitcast.295, s32[512]{0:T(512)S(1)} %bitcast.327, f32[512]{0:T(512)S(1)} %bitcast.271, s32[512]{0:T(512)S(1)} %bitcast.303, f32[512]{0:T(512)S(1)} %bitcast.275, s32[512]{0:T(512)S(1)} %bitcast.307, ...), kind=kOutput, calls=%fused_computation.44.clone.1 | convolution fusion | flops 233832448 | bytes 200704 | tf_op jit(solution)/shard_map/while/body/eval_jaxpr/dot_general | solution.py:127
  329.2 9.5 %fusion.315 = f32[8,16,512]{2,1,0:T(8,128)S(1)} fusion(f32[8,16,512]{2,1,0:T(8,128)S(1)} %get-tuple-element.431, s32[]{:T(128)S(6)} %copy.67, f32[512,16]{0,1:T(8,128)S(1)} %fusion.312, f32[512,16]{0,1:T(8,128)S(1)} %fusion.313, f32[512,16]{0,1:T(8,128)S(1)} %fusion.314, f32[16,2048]{1,0:T(8,128)S(1)} %get-tuple-element.453, f32[512]{0:T(512)S(1)} %bitcast.296, ...), kind=kOutput, calls=%fused_computation.220.clone.1 | convolution fusion | flops 233857024 | bytes 299012 | tf_op jit(solution)/shard_map/while/body/eval_jaxpr/dot_general | solution.py:127
  341.8 5.6 %collective-permute-start.7 = (f32[16,4,1,1024]{3,2,1,0:T(1,128)S(1)}, f32[16,4,1,1024]{3,2,1,0:T(1,128)S(1)}, u32[]{:S(2)}, u32[]{:S(2)}) collective-permute-start(f32[16,4,1,1024]{3,2,1,0:T(1,128)S(1)} %get-tuple-element.197), channel_id=1, source_target_pairs={{1,0},{2,1},{3,2},{4,3},{5,4},{6,5},{7,6},{8,7},{9,8},{10,9},{11,1... | collective-permute-start | bytes 786440 | tf_op jit(solution)/shard_map/ppermute | solution.py:31
  348.2 5.5 %collective-permute-done.8 = f32[16,4,1,1024]{3,2,1,0:T(1,128)S(1)} collective-permute-done((f32[16,4,1,1024]{3,2,1,0:T(1,128)S(1)}, f32[16,4,1,1024]{3,2,1,0:T(1,128)S(1)}, u32[]{:S(2)}, u32[]{:S(2)}) %collective-permute-start.8) | collective-permute-done | bytes 262176 | tf_op jit(solution)/shard_map/ppermute | solution.py:30
  354.9 2.2 multiply_add_fusion
  358.8 4.6 %collective-permute-start.9 = (f32[16,4,1,1024]{3,2,1,0:T(1,128)S(1)}, f32[16,4,1,1024]{3,2,1,0:T(1,128)S(1)}, u32[]{:S(2)}, u32[]{:S(2)}) collective-permute-start(f32[16,4,1,1024]{3,2,1,0:T(1,128)S(1)} %get-tuple-element.191), channel_id=1, source_target_pairs={{1,0},{2,1},{3,2},{4,3},{5,4},{6,5},{7,6},{8,7},{9,8},{10,9},{11,1... | collective-permute-start | bytes 786440 | tf_op jit(solution)/shard_map/ppermute | solution.py:31
  364.2 5.4 %collective-permute-done.10 = f32[16,4,1,1024]{3,2,1,0:T(1,128)S(1)} collective-permute-done((f32[16,4,1,1024]{3,2,1,0:T(1,128)S(1)}, f32[16,4,1,1024]{3,2,1,0:T(1,128)S(1)}, u32[]{:S(2)}, u32[]{:S(2)}) %collective-permute-start.10) | collective-permute-done | bytes 262176 | tf_op jit(solution)/shard_map/ppermute | solution.py:30
  370.4 3.0 add_bitcast_fusion
  (116 shorter events, 24.6 us)
Async XLA Ops:
  0.0 3.4 copy-start.4
  0.0 2.8 copy-start.9
  0.0 2.9 copy-start.10
  0.0 4.0 %copy-start.5 = (s32[1,8,4,1024]{3,2,1,0:T(4,128)S(1)}, s32[1,8,4,1024]{3,2,1,0:T(4,128)}, u32[]{:S(2)}) copy-start(s32[1,8,4,1024]{3,2,1,0:T(4,128)} %param.21) | copy-start | bytes 393220
  1.3 1.0 copy-start
  1.3 2.8 copy-start.6
  1.3 2.9 copy-start.7
  2.3 2.0 collective-permute-start.1
  2.8 1.4 collective-permute-start.2
  2.9 1.3 collective-permute-start
  18.6 9.5 %copy-start.8 = (s32[1,4,1024]{2,1,0:T(4,128)S(1)}, s32[1,4,1024]{2,1,0:T(4,128)}, u32[]{:S(2)}) copy-start(s32[1,4,1024]{2,1,0:T(4,128)} %param.18) | copy-start | bytes 49156
  19.2 11.0 %collective-permute-start.3 = (f32[16,2048]{1,0:T(8,128)S(1)}, f32[16,2048]{1,0:T(8,128)S(1)}, u32[]{:S(2)}, u32[]{:S(2)}) collective-permute-start(f32[16,2048]{1,0:T(8,128)S(1)} %bitcast.263), channel_id=1, source_target_pairs={{0,1},{1,2},{2,3},{3,4},{4,5},{5,6},{6,7},{7,8},{8,9},{9,10},{10,1... | collective-permute-start | bytes 393224 | tf_op jit(solution)/shard_map/ppermute | solution.py:20
  22.0 8.2 %collective-permute-start.4 = (f32[16,2048]{1,0:T(8,128)S(1)}, f32[16,2048]{1,0:T(8,128)S(1)}, u32[]{:S(2)}, u32[]{:S(2)}) collective-permute-start(f32[16,2048]{1,0:T(8,128)S(1)} %bitcast.262), channel_id=1, source_target_pairs={{0,0},{1,1},{2,2},{3,3},{4,4},{5,5},{6,6},{7,7},{8,8},{9,9},{10,10... | collective-permute-start | bytes 393224 | tf_op jit(solution)/shard_map/ppermute | solution.py:20
  22.0 8.1 %collective-permute-start.5 = (f32[16,2048]{1,0:T(8,128)S(1)}, f32[16,2048]{1,0:T(8,128)S(1)}, u32[]{:S(2)}, u32[]{:S(2)}) collective-permute-start(f32[16,2048]{1,0:T(8,128)S(1)} %bitcast.261), channel_id=1, source_target_pairs={{0,15},{1,0},{2,1},{3,2},{4,3},{5,4},{6,5},{7,6},{8,7},{9,8},{10,9... | collective-permute-start | bytes 393224 | tf_op jit(solution)/shard_map/ppermute | solution.py:20
  26.1 6.8 %collective-permute-start.6 = (f32[16,2048]{1,0:T(8,128)S(1)}, f32[16,2048]{1,0:T(8,128)S(1)}, u32[]{:S(2)}, u32[]{:S(2)}) collective-permute-start(f32[16,2048]{1,0:T(8,128)S(1)} %bitcast.260), channel_id=1, source_target_pairs={{0,14},{1,15},{2,0},{3,1},{4,2},{5,3},{6,4},{7,5},{8,6},{9,7},{10,... | collective-permute-start | bytes 393224 | tf_op jit(solution)/shard_map/ppermute | solution.py:20
  338.9 1.2 copy-start.1
  341.8 12.0 %collective-permute-start.8 = (f32[16,4,1,1024]{3,2,1,0:T(1,128)S(1)}, f32[16,4,1,1024]{3,2,1,0:T(1,128)S(1)}, u32[]{:S(2)}, u32[]{:S(2)}) collective-permute-start(f32[16,4,1,1024]{3,2,1,0:T(1,128)S(1)} %get-tuple-element.196), channel_id=1, source_target_pairs={{0,1},{1,2},{2,3},{3,4},{4,5},{5,6},{6,7},{7,8},{8,9},{9,10},{10,1... | collective-permute-start | bytes 786440 | tf_op jit(solution)/shard_map/ppermute | solution.py:30
  341.8 13.1 %copy-start.2 = (f32[4,4,1024]{2,1,0:T(4,128)S(1)}, f32[4,4,1024]{2,1,0:T(4,128)}, u32[]{:S(2)}) copy-start(f32[4,4,1024]{2,1,0:T(4,128)} %get-tuple-element.206) | copy-start | bytes 196612
  341.8 13.1 %copy-start.3 = (f32[4,4,1024]{2,1,0:T(4,128)S(1)}, f32[4,4,1024]{2,1,0:T(4,128)}, u32[]{:S(2)}) copy-start(f32[4,4,1024]{2,1,0:T(4,128)} %get-tuple-element.207) | copy-start | bytes 196612
  341.8 13.1 %collective-permute-start.7 = (f32[16,4,1,1024]{3,2,1,0:T(1,128)S(1)}, f32[16,4,1,1024]{3,2,1,0:T(1,128)S(1)}, u32[]{:S(2)}, u32[]{:S(2)}) collective-permute-start(f32[16,4,1,1024]{3,2,1,0:T(1,128)S(1)} %get-tuple-element.197), channel_id=1, source_target_pairs={{1,0},{2,1},{3,2},{4,3},{5,4},{6,5},{7,6},{8,7},{9,8},{10,9},{11,1... | collective-permute-start | bytes 786440 | tf_op jit(solution)/shard_map/ppermute | solution.py:31
  357.7 11.9 %collective-permute-start.10 = (f32[16,4,1,1024]{3,2,1,0:T(1,128)S(1)}, f32[16,4,1,1024]{3,2,1,0:T(1,128)S(1)}, u32[]{:S(2)}, u32[]{:S(2)}) collective-permute-start(f32[16,4,1,1024]{3,2,1,0:T(1,128)S(1)} %get-tuple-element.190), channel_id=1, source_target_pairs={{0,1},{1,2},{2,3},{3,4},{4,5},{5,6},{6,7},{7,8},{8,9},{9,10},{10,1... | collective-permute-start | bytes 786440 | tf_op jit(solution)/shard_map/ppermute | solution.py:30
  358.8 11.5 %collective-permute-start.9 = (f32[16,4,1,1024]{3,2,1,0:T(1,128)S(1)}, f32[16,4,1,1024]{3,2,1,0:T(1,128)S(1)}, u32[]{:S(2)}, u32[]{:S(2)}) collective-permute-start(f32[16,4,1,1024]{3,2,1,0:T(1,128)S(1)} %get-tuple-element.191), channel_id=1, source_target_pairs={{1,0},{2,1},{3,2},{4,3},{5,4},{6,5},{7,6},{8,7},{9,8},{10,9},{11,1... | collective-permute-start | bytes 786440 | tf_op jit(solution)/shard_map/ppermute | solution.py:31
where the time goes:
time: 374 us; the launch traced here: 373 us
  matrix products  316 us (84%)
  starting transfers between devices  21.3 us (6%)
  waiting for transfers between devices  17 us (5%)
  other arithmetic  9.5 us (3%)
  local copies, waits for them, and re-layouts  8.27 us (2%)
    dot_general x32, matrix products, remap_one_block(): jnp.dot(received[:, near], table, precision=lax.Precision.HIGHEST, prefer...  303 us
    dot_general x8, matrix products, pack_one_block(): jnp.einsum('qry,ys->qrs', surface, col_hot, precision=lax.Precision.HIGHE...  12.9 us
    ppermute x2, waiting for transfers between devices, with_halo(): before = lax.ppermute(last, axis, up)  10.9 us
    ppermute x2, starting transfers between devices, with_halo(): after = lax.ppermute(first, axis, down)  10.2 us
    ppermute x4, starting transfers between devices, passed_along(): return lax.ppermute(value, axis, pairs)  8.92 us
  transfers between devices with their start and end apart: 11, of which 6 were waited for; matrix products, arithmetic and copies ran while one was open for 1% of the time, Pallas kernels for 0%

commit v1 on v0

v1 whole, which is shorter than its diff:
```python
import functools

import jax
import jax.numpy as jnp
from jax import lax
from jax.experimental import pallas as pl
from jax.experimental.pallas import tpu as pltpu
from jax.sharding import PartitionSpec as P

diffusion = 0.12
LANES = 128
MESH = pl.DeviceIdType.MESH


def lane_pick(table, lanes):
    return jnp.take_along_axis(table, lanes, axis=1, mode="promise_in_bounds")


def pick_blocks(blocks, his, los, tracers):
    halves = tracers // 8
    picked = [[jnp.zeros((8, LANES), jnp.float32)] * halves for _ in his]
    for ident, load in blocks:
        parts = [load(half) for half in range(halves)]
        for n, (hi, lo) in enumerate(zip(his, los)):
            hit = hi == ident
            for half in range(halves):
                picked[n][half] = jnp.where(
                    hit, lane_pick(parts[half], lo), picked[n][half]
                )
    return picked


def exchange_kernel(
    dims,
    tracer_ref,
    vel_ref,
    coup_ref,
    mask_ref,
    rows_ref,
    cols_ref,
    near_ref,
    slot_ref,
    weight_ref,
    out_ref,
    lev_ref,
    vel_buf,
    packed,
    received,
    total,
    first,
    pack_send,
    pack_recv,
    halo_send,
    halo_recv,
    edge_send,
    edge_recv,
    vel_send,
    vel_recv,
):
    tiles, tracers, levels, rows, chunks, nears, blocks, inters = dims
    groups = rows * chunks
    halves = tracers // 8
    me_c = lax.axis_index("comp")
    me_t = lax.axis_index("tile")
    other = 1 - me_c

    def tile_at(step):
        return lax.rem(me_t + step + tiles, tiles)

    up, down = tile_at(1), tile_at(-1)
    steps = sorted({1 - j for j in range(nears)} | {j - 1 for j in range(nears)})
    barrier = pltpu.get_barrier_semaphore()
    for step in steps:
        pl.semaphore_signal(
            barrier, inc=1, device_id=(other, tile_at(step)), device_id_type=MESH
        )
    for side in (up, down):
        pl.semaphore_signal(barrier, inc=1, device_id=(me_c, side), device_id_type=MESH)

    def load_level(level):
        def one(g, _):
            c, r = g // rows, g % rows
            lev_ref[level, 2 + r, c] = tracer_ref[
                pl.ds(level * groups + g, tracers, stride=levels * groups), :
            ]
            return 0

        lax.fori_loop(0, groups, one, 0)

    load_level(0)

    def wide(ref, row):
        return jnp.broadcast_to(ref[pl.ds(row, 1), :], (8, LANES))

    def pack(j):
        batch = 4

        def one(b, _):
            his, los = [], []
            for n in range(batch):
                at = (b * batch + n) * nears + j
                row, col = wide(rows_ref, at), wide(cols_ref, at)
                his.append(row * chunks + (col >> 7))
                los.append(col & 127)
            table = [
                (
                    r * chunks + c,
                    lambda half, r=r, c=c: lev_ref[0, 2 + r, c, pl.ds(half * 8, 8), :],
                )
                for r in range(rows)
                for c in range(chunks)
            ]
            picked = pick_blocks(table, his, los, tracers)
            for n in range(batch):
                for half in range(halves):
                    packed[j, b * batch + n, pl.ds(half * 8, 8), :] = picked[n][half]
            return 0

        lax.fori_loop(0, blocks // batch, one, 0)

    order = [1] + [j for j in range(nears) if j != 1]
    pack_copies = {}
    for at, j in enumerate(order[1:] + order[:1]):
        pack(j)
        if at == 0:
            pl.semaphore_wait(barrier, len(steps) + 2)
        pack_copies[j] = pltpu.make_async_remote_copy(
            src_ref=packed.at[j],
            dst_ref=received.at[j],
            send_sem=pack_send.at[j],
            recv_sem=pack_recv.at[j],
            device_id=(other, tile_at(1 - j)),
            device_id_type=MESH,
        )
        pack_copies[j].start()

    for level in range(1, levels):
        load_level(level)

    def load_velocity(i, _):
        for c in range(chunks):
            for r in range(rows):
                vel_buf[1 + r, i, c] = vel_ref[pl.ds(i * groups + c * rows + r, 1), :]
        return 0

    lax.fori_loop(0, 2 * levels, load_velocity, 0)

    def to_side(src, dst, send, recv, side):
        copy = pltpu.make_async_remote_copy(
            src_ref=src,
            dst_ref=dst,
            send_sem=send,
            recv_sem=recv,
            device_id=(me_c, side),
            device_id_type=MESH,
        )
        copy.start()
        return copy

    inner = pl.ds(1, levels - 1)
    low, high = pl.ds(0, 2), pl.ds(rows + 2, 2)
    own_low, own_high = pl.ds(2, 2), pl.ds(rows, 2)
    side_copies = [
        to_side(
            lev_ref.at[inner, own_low],
            lev_ref.at[inner, high],
            halo_send.at[0],
            halo_recv.at[0],
            down,
        ),
        to_side(
            lev_ref.at[inner, own_high],
            lev_ref.at[inner, low],
            halo_send.at[1],
            halo_recv.at[1],
            up,
        ),
        to_side(
            vel_buf.at[1], vel_buf.at[rows + 1], vel_send.at[0], vel_recv.at[0], down
        ),
        to_side(vel_buf.at[rows], vel_buf.at[0], vel_send.at[1], vel_recv.at[1], up),
    ]

    def remap(r, c, nears_now):
        g = c * rows + r
        his, los = [], []
        for k in range(inters):
            near, slot = wide(near_ref, k * groups + g), wide(slot_ref, k * groups + g)
            his.append(near * blocks + (slot >> 7))
            los.append(slot & 127)
        table = [
            (
                j * blocks + b,
                lambda half, j=j, b=b: received[j, b, pl.ds(half * 8, 8), :],
            )
            for j in nears_now
            for b in range(blocks)
        ]
        picked = pick_blocks(table, his, los, tracers)
        sums = [jnp.zeros((8, LANES), jnp.float32)] * halves
        for k in range(inters):
            weight = wide(weight_ref, k * groups + g)
            sums = [sums[half] + weight * picked[k][half] for half in range(halves)]
        return sums

    def couple(r, c, sums):
        g = c * rows + r
        mask = wide(mask_ref, g).astype(jnp.float32)
        coup = coup_ref[pl.ds(g, tracers, stride=groups), :]
        for half in range(halves):
            at = pl.ds(half * 8, 8)
            old = lev_ref[0, 2 + r, c, at, :]
            part = coup[half * 8 : half * 8 + 8]
            lev_ref[0, 2 + r, c, at, :] = old + part * mask * (sums[half] - old)

    for at, j in enumerate(order):
        pack_copies[j].wait_recv()
        last = at == nears - 1

        def one(g, _, j=j, at=at, last=last):
            r, c = g // chunks, g % chunks
            sums = remap(r, c, [j])
            for half in range(halves):
                rows8 = pl.ds(half * 8, 8)
                if at > 0:
                    sums[half] = sums[half] + total[g, rows8, :]
                if not last:
                    total[g, rows8, :] = sums[half]
            if last:
                couple(r, c, sums)
            return 0

        lax.fori_loop(0, 2 * chunks, one, 0)
    edge_copies = [
        to_side(
            lev_ref.at[0, own_low],
            lev_ref.at[0, high],
            edge_send.at[0],
            edge_recv.at[0],
            down,
        )
    ]
    for r in range(2, rows):

        def one(c, _, r=r):
            couple(r, c, remap(r, c, order))
            return 0

        lax.fori_loop(0, chunks, one, 0)
        if r >= rows - 2:
            n = r - (rows - 2)
            edge_copies.append(
                to_side(
                    lev_ref.at[0, 2 + r],
                    lev_ref.at[0, n],
                    edge_send.at[1 + n],
                    edge_recv.at[1 + n],
                    up,
                )
            )

    lane = lax.broadcasted_iota(jnp.int32, (chunks * tracers, LANES), 1)

    def stepped(field, east, west, level, vrow):
        flat = field.reshape(chunks * tracers, LANES)
        ahead = pltpu.roll(flat, LANES - 1, 1)
        behind = pltpu.roll(flat, 1, 1)
        north = jnp.where(
            lane == LANES - 1,
            jnp.concatenate([ahead[tracers:], ahead[:tracers]], axis=0),
            ahead,
        ).reshape(chunks, tracers, LANES)
        south = jnp.where(
            lane == 0,
            jnp.concatenate([behind[-tracers:], behind[:-tracers]], axis=0),
            behind,
        ).reshape(chunks, tracers, LANES)
        u = vel_buf[vrow, level]
        v = vel_buf[vrow, levels + level]
        return (
            field
            - 0.5 * u * (east - west)
            - 0.5 * v * (north - south)
            + diffusion * (east + west + north + south - 4.0 * field)
        )

    def transport(level):
        def step_one(i, _):
            first[i] = stepped(
                lev_ref[level, i + 1],
                lev_ref[level, i + 2],
                lev_ref[level, i],
                level,
                i,
            )
            return 0

        lax.fori_loop(0, rows + 2, step_one, 0)

        def step_two(r, _):
            value = stepped(first[r + 1], first[r + 2], first[r], level, r + 1)
            for c in range(chunks):
                out_ref[
                    pl.ds(
                        level * groups + c * rows + r, tracers, stride=levels * groups
                    ),
                    :,
                ] = value[c]
            return 0

        lax.fori_loop(0, rows, step_two, 0)

    for copy in side_copies:
        copy.wait()

    def inner_level(level, _):
        transport(level)
        return 0

    lax.fori_loop(1, levels, inner_level, 0)
    for copy in edge_copies:
        copy.wait()
    transport(0)
    for j in order:
        pack_copies[j].wait_send()


def split_rows(x):
    *lead, rows, width = x.shape
    chunks = width // LANES
    x = jnp.swapaxes(x.reshape(*lead, rows, chunks, LANES), -3, -2)
    return x.reshape(-1, LANES)


def per_device(
    tiles,
    tracer,
    velocity,
    coupling,
    sea_mask,
    send_rows,
    send_cols,
    intersection_near,
    intersection_slot,
    intersection_weight,
):
    _, tracers, levels, rows, width = tracer.shape
    nears, capacity = send_rows.shape[2:]
    inters = intersection_slot.shape[1]
    chunks, blocks = width // LANES, capacity // LANES
    dims = (tiles, tracers, levels, rows, chunks, nears, blocks, inters)
    dma = pltpu.SemaphoreType.DMA
    vmem = pl.BlockSpec(memory_space=pltpu.VMEM)
    f32 = jnp.float32
    out = pl.pallas_call(
        functools.partial(exchange_kernel, dims),
        out_shape=jax.ShapeDtypeStruct((tracers * levels * rows * chunks, LANES), f32),
        in_specs=[vmem] * 9,
        out_specs=vmem,
        scratch_shapes=[
            pltpu.VMEM((levels, rows + 4, chunks, tracers, LANES), f32),
            pltpu.VMEM((rows + 2, 2 * levels, chunks, 1, LANES), f32),
            pltpu.VMEM((nears, blocks, tracers, LANES), f32),
            pltpu.VMEM((nears, blocks, tracers, LANES), f32),
            pltpu.VMEM((2 * chunks, tracers, LANES), f32),
            pltpu.VMEM((rows + 2, chunks, tracers, LANES), f32),
            dma((nears,)),
            dma((nears,)),
            dma((2,)),
            dma((2,)),
            dma((3,)),
            dma((3,)),
            dma((2,)),
            dma((2,)),
        ],
        compiler_params=pltpu.CompilerParams(collective_id=0, has_side_effects=True),
    )(
        split_rows(tracer),
        split_rows(velocity),
        split_rows(coupling),
        split_rows(sea_mask),
        split_rows(send_rows),
        split_rows(send_cols),
        split_rows(intersection_near),
        split_rows(intersection_slot),
        split_rows(intersection_weight),
    )
    out = out.reshape(1, tracers, levels, chunks, rows, LANES)
    return jnp.swapaxes(out, 3, 4).reshape(tracer.shape)


def solution(mesh):
    in_specs = (
        P("comp", None, None, "tile", None),
        P("comp", None, None, "tile", None),
        P("comp", None, "tile", None),
        P("comp", "tile", None),
        P("comp", "tile", None, None),
        P("comp", "tile", None, None),
        P("comp", None, "tile", None),
        P("comp", None, "tile", None),
        P("comp", None, "tile", None),
    )
    out_specs = P("comp", None, None, "tile", None)
    return jax.shard_map(
        functools.partial(per_device, mesh.shape["tile"]),
        mesh=mesh,
        in_specs=in_specs,
        out_specs=out_specs,
        check_vma=False,
    )
```

time: 374 us -> 115 us (0.31)
  matrix products: 316 us -> 0 us
  Pallas kernels: 0 us -> 113 us
  starting transfers between devices: 21.3 us -> 0 us
  waiting for transfers between devices: 17 us -> 0 us
  other arithmetic: 9.5 us -> 0 us
  local copies, waits for them, and re-layouts: 8.27 us -> 2.29 us
    dot_general x40 -> x0, matrix products: 316 us -> none  [the longest x32 303 us: remap_one_block(): jnp.dot(received[:, near], table, precision=lax.Precision.HIGHEST, prefer...]
    pallas_call x0 -> x1, Pallas kernels: none -> 113 us  [per_device(): pl.pallas_call(functools.partial(exchange_kernel, dims), out_shape=jax.Sh...]
    ppermute x11 -> x0, starting transfers between devices: 21.3 us -> none  [the longest x2 10.2 us: with_halo(): after = lax.ppermute(first, axis, down)]
    ppermute x11 -> x0, waiting for transfers between devices: 17 us -> none  [the longest x2 10.9 us: with_halo(): before = lax.ppermute(last, axis, up)]
  transfers between devices with their start and end apart: 11 -> 0, of which waited for: 6 -> 0; matrix products, arithmetic and copies ran while one was open for 1% -> 0% of each run, Pallas kernels for 0% -> 0%
where the time goes in v1:
time: 115 us
  Pallas kernels  113 us (98%)
  local copies, waits for them, and re-layouts  2.29 us (2%)
    pallas_call x1, Pallas kernels, per_device(): pl.pallas_call(functools.partial(exchange_kernel, dims), out_shape=jax.Sh...  113 us

profile of v1, /device:TPU:0, one launch (start us, length us, event | category | flops | bytes accessed | tf_op | source)
XLA Modules:
  0.0 114.9 jit_solution(7025459503106218479)
XLA Ops:
  0.0 112.7 %shard_map.91 = f32[2048,128]{1,0:T(8,128)} custom-call(f32[2048,128]{1,0:T(8,128)} %bitcast.51, f32[256,128]{1,0:T(8,128)} %bitcast.53, f32[512,128]{1,0:T(8,128)} %bitcast.52, s32[32,128]{1,0:T(8,128)} %bitcast.59, s32[64,128]{1,0:T(8,128)} %bitcast.57, s32[64,128]{1,0:T(8,128)} %bitcast.58, s32[256,128]{1,0:T(8,128)} %bitcast.54, s32[256,128]{1,0:T(8,128)} %bitcast.55, ...), custom_call_target="tpu_custom_call" | custom-call | tf_op jit(solution)/shard_map/pallas_call | solution.py:355
  112.7 2.3 %copy.21 = f32[1,16,4,4,1024]{4,3,2,1,0:T(4,128)} copy(f32[1,16,4,4,1024]{4,3,2,1,0:T(4,128)} %bitcast.50) | data formatting | bytes 2097152

commit v2 on v1

--- a/solution.py
+++ b/solution.py
@@ -18,15 +18,15 @@
 
 def pick_blocks(blocks, his, los, tracers):
     halves = tracers // 8
-    picked = [[jnp.zeros((8, LANES), jnp.float32)] * halves for _ in his]
-    for ident, load in blocks:
-        parts = [load(half) for half in range(halves)]
-        for n, (hi, lo) in enumerate(zip(his, los)):
+    picked = []
+    for hi, lo in zip(his, los):
+        chains = [[jnp.zeros((8, LANES), jnp.float32)] * 2 for _ in range(halves)]
+        for n, (ident, load) in enumerate(blocks):
             hit = hi == ident
             for half in range(halves):
-                picked[n][half] = jnp.where(
-                    hit, lane_pick(parts[half], lo), picked[n][half]
-                )
+                chain = chains[half]
+                chain[n % 2] = jnp.where(hit, lane_pick(load(half), lo), chain[n % 2])
+        picked.append([one + two for one, two in chains])
     return picked
 
 

time: 115 us -> 66.7 us (0.58)
  Pallas kernels: 113 us -> 64.3 us
    pallas_call x1, Pallas kernels: 113 us -> 64.3 us  [per_device(): pl.pallas_call(functools.partial(exchange_kernel, dims), out_shape=jax.Sh...]
where the time goes in v2:
time: 66.7 us; the launch traced here: 66.6 us
  Pallas kernels  64.3 us (96%)
  local copies, waits for them, and re-layouts  2.29 us (3%)
    pallas_call x1, Pallas kernels, per_device(): pl.pallas_call(functools.partial(exchange_kernel, dims), out_shape=jax.Sh...  64.3 us
    unnamed x1, local copies, waits for them, and re-layouts  2.29 us

profile of v2, /device:TPU:0, one launch (start us, length us, event | category | flops | bytes accessed | tf_op | source)
XLA Modules:
  0.0 66.6 jit_solution(12363331765117529878)
XLA Ops:
  0.0 64.3 %shard_map.91 = f32[2048,128]{1,0:T(8,128)} custom-call(f32[2048,128]{1,0:T(8,128)} %bitcast.51, f32[256,128]{1,0:T(8,128)} %bitcast.53, f32[512,128]{1,0:T(8,128)} %bitcast.52, s32[32,128]{1,0:T(8,128)} %bitcast.59, s32[64,128]{1,0:T(8,128)} %bitcast.57, s32[64,128]{1,0:T(8,128)} %bitcast.58, s32[256,128]{1,0:T(8,128)} %bitcast.54, s32[256,128]{1,0:T(8,128)} %bitcast.55, ...), custom_call_target="tpu_custom_call" | custom-call | tf_op jit(solution)/shard_map/pallas_call | solution.py:355
  64.3 2.3 %copy.21 = f32[1,16,4,4,1024]{4,3,2,1,0:T(4,128)} copy(f32[1,16,4,4,1024]{4,3,2,1,0:T(4,128)} %bitcast.50) | data formatting | bytes 2097152

commit v3 on v2

--- a/solution.py
+++ b/solution.py
@@ -10,6 +10,8 @@
 diffusion = 0.12
 LANES = 128
 MESH = pl.DeviceIdType.MESH
+PAIR = 2
+ON_LANES = 2
 
 
 def lane_pick(table, lanes):
@@ -27,6 +29,41 @@
                 chain = chains[half]
                 chain[n % 2] = jnp.where(hit, lane_pick(load(half), lo), chain[n % 2])
         picked.append([one + two for one, two in chains])
+    return picked
+
+
+def split_pieces(value, pieces, block, tracers):
+    top = value.astype(jnp.bfloat16)
+    rest = (value - top.astype(jnp.float32)).astype(jnp.bfloat16)
+    rows_at = pl.ds(block * tracers, tracers)
+    pieces[rows_at, pl.ds(0, LANES)] = top
+    pieces[rows_at, pl.ds(LANES, LANES)] = rest
+
+
+def dot_blocks(left, his, los, tracers):
+    halves = tracers // 8
+    count = left.shape[0] // tracers
+    lane_id = lax.broadcasted_iota(jnp.int32, (LANES, LANES), 0)
+    picked = []
+    for k in range(0, len(his), PAIR):
+        hots = []
+        for lo in los[k : k + PAIR]:
+            hot = lane_id == jnp.broadcast_to(lo, (LANES, LANES))
+            hot = hot.astype(jnp.float32).astype(jnp.bfloat16)
+            hots.append(jnp.concatenate([hot, hot], axis=0))
+        found = jnp.dot(
+            left, jnp.concatenate(hots, axis=1), preferred_element_type=jnp.float32
+        )
+        for n, hi in enumerate(his[k : k + PAIR]):
+            hi = jnp.broadcast_to(hi, (8, LANES))
+            part = [jnp.zeros((8, LANES), jnp.float32)] * halves
+            for block in range(count):
+                hit = hi == block
+                for half in range(halves):
+                    row = block * tracers + half * 8
+                    cell = found[row : row + 8, n * LANES : (n + 1) * LANES]
+                    part[half] = jnp.where(hit, cell, part[half])
+            picked.append(part)
     return picked
 
 
@@ -46,8 +83,9 @@
     vel_buf,
     packed,
     received,
-    total,
     first,
+    pieces,
+    surface_pieces,
     pack_send,
     pack_recv,
     halo_send,
@@ -92,6 +130,10 @@
     def wide(ref, row):
         return jnp.broadcast_to(ref[pl.ds(row, 1), :], (8, LANES))
 
+    for r in range(rows):
+        for c in range(chunks):
+            split_pieces(lev_ref[0, 2 + r, c], surface_pieces, r * chunks + c, tracers)
+
     def pack(j):
         batch = 4
 
@@ -99,18 +141,10 @@
             his, los = [], []
             for n in range(batch):
                 at = (b * batch + n) * nears + j
-                row, col = wide(rows_ref, at), wide(cols_ref, at)
+                row, col = rows_ref[pl.ds(at, 1), :], cols_ref[pl.ds(at, 1), :]
                 his.append(row * chunks + (col >> 7))
                 los.append(col & 127)
-            table = [
-                (
-                    r * chunks + c,
-                    lambda half, r=r, c=c: lev_ref[0, 2 + r, c, pl.ds(half * 8, 8), :],
-                )
-                for r in range(rows)
-                for c in range(chunks)
-            ]
-            picked = pick_blocks(table, his, los, tracers)
+            picked = dot_blocks(surface_pieces[...], his, los, tracers)
             for n in range(batch):
                 for half in range(halves):
                     packed[j, b * batch + n, pl.ds(half * 8, 8), :] = picked[n][half]
@@ -181,26 +215,34 @@
         to_side(vel_buf.at[rows], vel_buf.at[0], vel_send.at[1], vel_recv.at[1], up),
     ]
 
-    def remap(r, c, nears_now):
+    def remap(r, c):
         g = c * rows + r
-        his, los = [], []
-        for k in range(inters):
-            near, slot = wide(near_ref, k * groups + g), wide(slot_ref, k * groups + g)
-            his.append(near * blocks + (slot >> 7))
-            los.append(slot & 127)
         table = [
             (
                 j * blocks + b,
                 lambda half, j=j, b=b: received[j, b, pl.ds(half * 8, 8), :],
             )
-            for j in nears_now
+            for j in range(nears)
             for b in range(blocks)
         ]
-        picked = pick_blocks(table, his, los, tracers)
+        his, los, weights = [], [], []
+        for k in range(inters):
+            at = k * groups + g
+            his.append(near_ref[pl.ds(at, 1), :] * blocks + (slot_ref[pl.ds(at, 1), :] >> 7))
+            los.append(slot_ref[pl.ds(at, 1), :] & 127)
+            weights.append(wide(weight_ref, at))
+        on_mxu = inters - ON_LANES
+        picked = dot_blocks(pieces[...], his[:on_mxu], los[:on_mxu], tracers)
+        if ON_LANES > 0:
+            picked += pick_blocks(
+                table,
+                [jnp.broadcast_to(x, (8, LANES)) for x in his[on_mxu:]],
+                [jnp.broadcast_to(x, (8, LANES)) for x in los[on_mxu:]],
+                tracers,
+            )
         sums = [jnp.zeros((8, LANES), jnp.float32)] * halves
-        for k in range(inters):
-            weight = wide(weight_ref, k * groups + g)
-            sums = [sums[half] + weight * picked[k][half] for half in range(halves)]
+        for weight, part in zip(weights, picked):
+            sums = [sums[half] + weight * part[half] for half in range(halves)]
         return sums
 
     def couple(r, c, sums):
@@ -213,24 +255,21 @@
             part = coup[half * 8 : half * 8 + 8]
             lev_ref[0, 2 + r, c, at, :] = old + part * mask * (sums[half] - old)
 
-    for at, j in enumerate(order):
+    for j in order[1:] + order[:1]:
         pack_copies[j].wait_recv()
-        last = at == nears - 1
-
-        def one(g, _, j=j, at=at, last=last):
-            r, c = g // chunks, g % chunks
-            sums = remap(r, c, [j])
-            for half in range(halves):
-                rows8 = pl.ds(half * 8, 8)
-                if at > 0:
-                    sums[half] = sums[half] + total[g, rows8, :]
-                if not last:
-                    total[g, rows8, :] = sums[half]
-            if last:
-                couple(r, c, sums)
-            return 0
-
-        lax.fori_loop(0, 2 * chunks, one, 0)
+
+    def split_slots(b, _):
+        for j in range(nears):
+            split_pieces(received[j, b], pieces, j * blocks + b, tracers)
+        return 0
+
+    lax.fori_loop(0, blocks, split_slots, 0)
+
+    def low_rows(g, _):
+        couple(g // chunks, g % chunks, remap(g // chunks, g % chunks))
+        return 0
+
+    lax.fori_loop(0, 2 * chunks, low_rows, 0)
     edge_copies = [
         to_side(
             lev_ref.at[0, own_low],
@@ -243,7 +282,7 @@
     for r in range(2, rows):
 
         def one(c, _, r=r):
-            couple(r, c, remap(r, c, order))
+            couple(r, c, remap(r, c))
             return 0
 
         lax.fori_loop(0, chunks, one, 0)
@@ -295,7 +334,7 @@
             )
             return 0
 
-        lax.fori_loop(0, rows + 2, step_one, 0)
+        lax.fori_loop(0, rows + 2, step_one, 0, unroll=2)
 
         def step_two(r, _):
             value = stepped(first[r + 1], first[r + 2], first[r], level, r + 1)
@@ -308,7 +347,7 @@
                 ] = value[c]
             return 0
 
-        lax.fori_loop(0, rows, step_two, 0)
+        lax.fori_loop(0, rows, step_two, 0, unroll=2)
 
     for copy in side_copies:
         copy.wait()
@@ -362,8 +401,9 @@
             pltpu.VMEM((rows + 2, 2 * levels, chunks, 1, LANES), f32),
             pltpu.VMEM((nears, blocks, tracers, LANES), f32),
             pltpu.VMEM((nears, blocks, tracers, LANES), f32),
-            pltpu.VMEM((2 * chunks, tracers, LANES), f32),
             pltpu.VMEM((rows + 2, chunks, tracers, LANES), f32),
+            pltpu.VMEM((nears * blocks * tracers, 2 * LANES), jnp.bfloat16),
+            pltpu.VMEM((rows * chunks * tracers, 2 * LANES), jnp.bfloat16),
             dma((nears,)),
             dma((nears,)),
             dma((2,)),

time: 66.7 us -> 50.2 us (0.75)
  the two profiles are of different devices: /device:TPU:0 before, /device:TPU:5 now
where the time goes in v3:
time: 50.2 us; the launch traced here: 50 us
  Pallas kernels  47.7 us (95%)
  local copies, waits for them, and re-layouts  2.29 us (5%)
    pallas_call x1, Pallas kernels, per_device(): pl.pallas_call(functools.partial(exchange_kernel, dims), out_shape=jax.Sh...  47.7 us
    unnamed x1, local copies, waits for them, and re-layouts  2.29 us

profile of v3, /device:TPU:5, one launch (start us, length us, event | category | flops | bytes accessed | tf_op | source)
XLA Modules:
  0.0 50.0 jit_solution(8301108734878661656)
XLA Ops:
  0.0 47.7 %shard_map.91 = f32[2048,128]{1,0:T(8,128)} custom-call(f32[2048,128]{1,0:T(8,128)} %bitcast.51, f32[256,128]{1,0:T(8,128)} %bitcast.53, f32[512,128]{1,0:T(8,128)} %bitcast.52, s32[32,128]{1,0:T(8,128)} %bitcast.59, s32[64,128]{1,0:T(8,128)} %bitcast.57, s32[64,128]{1,0:T(8,128)} %bitcast.58, s32[256,128]{1,0:T(8,128)} %bitcast.54, s32[256,128]{1,0:T(8,128)} %bitcast.55, ...), custom_call_target="tpu_custom_call" | custom-call | tf_op jit(solution)/shard_map/pallas_call | solution.py:394
  47.7 2.3 %copy.21 = f32[1,16,4,4,1024]{4,3,2,1,0:T(4,128)} copy(f32[1,16,4,4,1024]{4,3,2,1,0:T(4,128)} %bitcast.50) | data formatting | bytes 2097152

commit v4 on v3

--- a/solution.py
+++ b/solution.py
@@ -135,7 +135,7 @@
             split_pieces(lev_ref[0, 2 + r, c], surface_pieces, r * chunks + c, tracers)
 
     def pack(j):
-        batch = 4
+        batch = 8
 
         def one(b, _):
             his, los = [], []
@@ -144,7 +144,22 @@
                 row, col = rows_ref[pl.ds(at, 1), :], cols_ref[pl.ds(at, 1), :]
                 his.append(row * chunks + (col >> 7))
                 los.append(col & 127)
-            picked = dot_blocks(surface_pieces[...], his, los, tracers)
+            on_mxu = batch - 2
+            picked = dot_blocks(surface_pieces[...], his[:on_mxu], los[:on_mxu], tracers)
+            table = [
+                (
+                    r * chunks + c,
+                    lambda half, r=r, c=c: lev_ref[0, 2 + r, c, pl.ds(half * 8, 8), :],
+                )
+                for r in range(rows)
+                for c in range(chunks)
+            ]
+            picked += pick_blocks(
+                table,
+                [jnp.broadcast_to(x, (8, LANES)) for x in his[on_mxu:]],
+                [jnp.broadcast_to(x, (8, LANES)) for x in los[on_mxu:]],
+                tracers,
+            )
             for n in range(batch):
                 for half in range(halves):
                     packed[j, b * batch + n, pl.ds(half * 8, 8), :] = picked[n][half]
@@ -269,7 +284,7 @@
         couple(g // chunks, g % chunks, remap(g // chunks, g % chunks))
         return 0
 
-    lax.fori_loop(0, 2 * chunks, low_rows, 0)
+    lax.fori_loop(0, 2 * chunks, low_rows, 0, unroll=2)
     edge_copies = [
         to_side(
             lev_ref.at[0, own_low],
@@ -285,7 +300,7 @@
             couple(r, c, remap(r, c))
             return 0
 
-        lax.fori_loop(0, chunks, one, 0)
+        lax.fori_loop(0, chunks, one, 0, unroll=2)
         if r >= rows - 2:
             n = r - (rows - 2)
             edge_copies.append(

time: 50.2 us -> 46.4 us (0.924)
  the two profiles are of different devices: /device:TPU:5 before, /device:TPU:13 now
where the time goes in v4:
time: 46.4 us; the launch traced here: 46.3 us
  Pallas kernels  44 us (95%)
  local copies, waits for them, and re-layouts  2.29 us (5%)
    pallas_call x1, Pallas kernels, per_device(): pl.pallas_call(functools.partial(exchange_kernel, dims), out_shape=jax.Sh...  44 us
    unnamed x1, local copies, waits for them, and re-layouts  2.29 us

profile of v4, /device:TPU:13, one launch (start us, length us, event | category | flops | bytes accessed | tf_op | source)
XLA Modules:
  0.0 46.3 jit_solution(3801912652614258511)
XLA Ops:
  0.0 44.0 %shard_map.91 = f32[2048,128]{1,0:T(8,128)} custom-call(f32[2048,128]{1,0:T(8,128)} %bitcast.51, f32[256,128]{1,0:T(8,128)} %bitcast.53, f32[512,128]{1,0:T(8,128)} %bitcast.52, s32[32,128]{1,0:T(8,128)} %bitcast.59, s32[64,128]{1,0:T(8,128)} %bitcast.57, s32[64,128]{1,0:T(8,128)} %bitcast.58, s32[256,128]{1,0:T(8,128)} %bitcast.54, s32[256,128]{1,0:T(8,128)} %bitcast.55, ...), custom_call_target="tpu_custom_call" | custom-call | tf_op jit(solution)/shard_map/pallas_call | solution.py:409
  44.0 2.3 %copy.21 = f32[1,16,4,4,1024]{4,3,2,1,0:T(4,128)} copy(f32[1,16,4,4,1024]{4,3,2,1,0:T(4,128)} %bitcast.50) | data formatting | bytes 2097152
